TPU v7x, 1024 devices: a whole 8x8x8 slice. The times are simulated.
1024 devices in a mesh: gx: 16 (over y, z_lo), gy: 8 (over x), gz: 8 (over z_hi, core).
Axes of the slice: x: 8, y: 8, z: 8 (z_hi: 4, z_lo: 2; z = z_hi * 2 + z_lo), core: 2. Of those that a mesh axis runs over, the one named last changes fastest.
Arguments:
- positions: float32 [3, 16, 8, 8, 512], P(None, 'gx', 'gy', 'gz'), may hold values from 0 to 1
- velocities: float32 [3, 16, 8, 8, 512], P(None, 'gx', 'gy', 'gz'), may hold values from -1.8 to 1.8
- forces: float32 [3, 16, 8, 8, 512], P(None, 'gx', 'gy', 'gz'), may hold values from -6 to 6
- charges: float32 [16, 8, 8, 512], P('gx', 'gy', 'gz'), may hold values from -4 to 4
- atom_types: int32 [16, 8, 8, 512], P('gx', 'gy', 'gz'), may hold values from 0 to 31
- tile_counts: int32 [16, 8, 8], P('gx', 'gy', 'gz'), may hold values from 1 to 4, as said below
- pair_epsilon: float32 [32], replicated, may hold values from 0.01 to 0.1
- pair_sigma: float32 [32], replicated, may hold values from 0.1 to 0.15
Outputs:
- final_positions: float32 [3, 16, 8, 8, 512], P(None, 'gx', 'gy', 'gz')
- final_velocities: float32 [3, 16, 8, 8, 512], P(None, 'gx', 'gy', 'gz')
- final_forces: float32 [3, 16, 8, 8, 512], P(None, 'gx', 'gy', 'gz')
Inputs may be any that keep to these rules, and one draw needn't show every extreme that they name: The live atoms of a box are its first 128 times tile_counts slots; some box has 4 live tiles in every draw.
All inputs are finite; a program needn't handle non-finite values.
Results may differ from a plain program's by a relative error of at most 0.0003.
Values sent between devices are 32-bit elements; how exact they have to be, the bound alone decides.
A program may use at most 32 MiB of HBM per device.

v0:
```python
import functools

import jax
import jax.numpy as jnp
from jax import lax
from jax.experimental import pallas as pl
from jax.experimental.pallas import tpu as pltpu
from jax.sharding import PartitionSpec as P

TILE = 128
STEPS = 2
TIME_STEP = 0.05
HALF_STEP = 0.025
PLATE = ((1, 0), (1, 1), (0, 1), (-1, 1), (-1, 0), (-1, -1), (0, -1), (1, -1))
NP = len(PLATE)
OFFSETS = tuple((x, y, 0) for x, y in PLATE) + ((0, 0, -1), (0, 0, 1))
NBR = NP + 2
AXES = ("gx", "gy", "gz")
MESH = pl.DeviceIdType.MESH
F32 = jnp.float32
BF16 = jnp.bfloat16
FAR = 1e6
RIGHTS = 4 * (NP + 2)
RROWS = RIGHTS + 8
UNROLL = 8
PAD = 12
LOG2E = 1.4426950408889634
FORCE = 8.0 / (3.24 * 3.24)


def shares(first, pos_ref, par_ref, own_ref):
    row = lax.broadcasted_iota(jnp.int32, (64, TILE), 0)
    col = lax.broadcasted_iota(jnp.int32, (64, TILE), 1)
    lane = lax.broadcasted_iota(jnp.int32, (1, TILE), 1) >> 2
    lt, lbox, rt, rbox = row >> 4, (row >> 2) & 3, col & 3, col >> 2
    own_n = par_ref[NBR, 1, 12:13, :]
    nr = own_n
    for j in range(NP):
        nr = jnp.where(lane == j, par_ref[j, 1, 12:13, :], nr)
    below_n, above_n = par_ref[NP, 1, 12:13, :], par_ref[NP + 1, 1, 12:13, :]
    nl = jnp.where(lbox == 0, below_n, jnp.where(lbox == 2, above_n, own_n))
    nr = jnp.broadcast_to(nr, (64, TILE))
    ahead = (rbox < NP // 2) | ((rbox == NP) & (lbox == 2))
    left_first = (rbox < NP // 2) | ((rbox == NP) & (lbox == 0))
    lf, rf = lt.astype(F32), rt.astype(F32)
    order = jnp.where(left_first, lf * nr + rf, rf * nl + lf)
    if first:
        w1 = jnp.where(left_first, nl, nr)
        w2 = jnp.where(left_first, nr, nl)
    else:
        mine = own_ref[14:15, :]
        below, same, above = mine, mine, mine
        for j in range(NP):
            hit = lane == j
            below = jnp.where(hit, pos_ref[j, 12:13, :], below)
            same = jnp.where(hit, pos_ref[j, 14:15, :], same)
            above = jnp.where(hit, pos_ref[j, 13:14, :], above)
        below = jnp.where(lane == NP, pos_ref[NP, 14:15, :], below)
        above = jnp.where(lane == NP, pos_ref[NP + 1, 14:15, :], above)
        other = jnp.where(lbox == 0, below, jnp.where(lbox == 2, above, same))
        mine = jnp.broadcast_to(mine, (64, TILE))
        w1 = jnp.where(ahead, mine, other)
        w2 = jnp.where(ahead, other, mine)
    w1, w2 = w1 * w1 * w1, w2 * w2 * w2
    inside = (order + 0.5) * (w1 + w2) < w2 * (nl * nr)
    takes = jnp.where(inside, 1.0, 0.0)
    takes = jnp.where(ahead, takes, 1.0 - takes)
    shared = ((rbox < NP) & (lbox < 3)) | ((rbox == NP) & ((lbox == 0) | (lbox == 2)))
    alone = ((rbox == NP) & (lbox == 1) & (lt < rt)) | ((rbox == NP + 1) & (lbox == 1) & (lt == rt))
    return jnp.where(shared, takes, jnp.where(alone, 1.0, -1.0))


def pair_kernel(
    joined, pos_ref, par_ref, own_ref, fout_ref, fown_ref,
    left, right, acc_left, acc_right, list_v, list_s, sem,
):
    position = (lambda k: pos_ref[k, 0]) if joined else (lambda k: pos_ref[k])
    own = own_ref[NBR, 0] if joined else own_ref[...]
    row16 = lax.broadcasted_iota(jnp.int32, (16, 1), 0)
    lane16 = lax.broadcasted_iota(jnp.int32, (1, 16), 1)
    for k in range(NP + 2):
        if k < NP:
            p = position(k) + jnp.where(
                row16 < 4, float(PLATE[k][0]), jnp.where(row16 < 8, float(PLATE[k][1]), 0.0)
            )
            a = par_ref[k, 1]
        else:
            p, a = own, par_ref[NBR, 1]
        p = p * 2.0
        for f in range(3):
            right[f, 4 * k : 4 * k + 4, :] = p[4 * f : 4 * f + 4]
            right[3 + f, 4 * k : 4 * k + 4, :] = a[4 * f : 4 * f + 4]
    for f in range(6):
        right[f, RIGHTS:RROWS, :] = jnp.full((8, TILE), FAR if f < 3 else 0.0, F32)
    mins, maxs, downs = [], [], []
    scale = jnp.where(lane16 < 4, 0.04 / 6.0 * FORCE, jnp.where(lane16 < 8, 4.0 * FORCE, 1.0))
    for box in range(3):
        if box == 1:
            p, a = own, par_ref[NBR, 1]
        else:
            slot = NP if box == 0 else NP + 1
            p = position(slot) + jnp.where(
                (row16 >= 8) & (row16 < 12), -1.0 if box == 0 else 1.0, 0.0
            )
            a = par_ref[slot, 1]
        down = jnp.transpose(jnp.concatenate([p * 2.0, a], 0), (1, 0))
        blocks = down[:, :16].reshape(4, 32, 16)
        mins.append(jnp.min(blocks, axis=1))
        maxs.append(jnp.max(blocks, axis=1))
        downs.append(down)
    far = jnp.full((4, 16), FAR, F32)
    low = jnp.concatenate(mins + [far], 0)
    high = jnp.concatenate(maxs + [far], 0)
    gaps = jnp.zeros((64, TILE), F32)
    alive = None
    for f in range(3):
        a0 = jnp.concatenate([low[:, 4 * f + t : 4 * f + t + 1] for t in range(4)], 0)
        a1 = jnp.concatenate([high[:, 4 * f + t : 4 * f + t + 1] for t in range(4)], 0)
        v = jnp.concatenate([right[f], jnp.full((TILE - RROWS, TILE), FAR, F32)], 0)
        b0 = jnp.broadcast_to(jnp.min(v, axis=1, keepdims=True), (TILE, TILE))
        b1 = jnp.broadcast_to(jnp.max(v, axis=1, keepdims=True), (TILE, TILE))
        b0 = jnp.transpose(b0, (1, 0))[:1]
        b1 = jnp.transpose(b1, (1, 0))[:1]
        gap = jnp.maximum(jnp.maximum(a0 - b1, b0 - a1), 0.0)
        gaps = gaps + gap * gap
        if f == 0:
            alive = a0 < 0.1 * FAR
    mine = shares(joined, pos_ref, par_ref, own_ref)
    close = (gaps < 3.2401) & alive
    near = close & (mine > 0.5)
    weight = jnp.sum(jnp.where(close & (mine > -0.5), 1.0, 0.0), axis=0, keepdims=True)
    weight = jnp.sum(weight, axis=1, keepdims=True) + 1.0
    row = lax.broadcasted_iota(jnp.int32, (64, TILE), 0)
    r64 = lax.broadcasted_iota(jnp.int32, (64, 64), 0)
    c64 = lax.broadcasted_iota(jnp.int32, (64, 64), 1)
    ones = near.astype(F32)
    before = jnp.dot(
        (c64 < r64).astype(F32).astype(BF16), ones.astype(BF16), preferred_element_type=F32
    )
    place = jnp.where(near, before.astype(jnp.int32), -1)
    lane = lax.broadcasted_iota(jnp.int32, (1, TILE), 1)
    count = jnp.maximum(jnp.sum(ones, axis=0, keepdims=True), 1.0)
    total = jnp.sum(jnp.where(lane < RIGHTS, count, 0.0), axis=1, keepdims=True)
    count = jnp.where(lane < RIGHTS, count, 1e6).astype(jnp.int32)
    value = row - PAD
    for w in range(12):
        word = jnp.zeros((1, TILE), jnp.int32)
        for j in range(4):
            hit = jnp.where(place == 4 * w + j, value, 0)
            word = word + (jnp.sum(hit, axis=0, keepdims=True) + PAD) * (64**j)
        list_v[w : w + 1, :] = word
    list_v[12:13, :] = count
    list_v[13:14, :] = jnp.broadcast_to(total, (1, TILE)).astype(jnp.int32)
    copy = pltpu.make_async_copy(list_v, list_s, sem)
    copy.start()
    for box, down in enumerate(downs):
        scaled = down[:, 16:] * scale
        for t in range(4):
            base = (t * 16 + box * 4) * 4
            for f in range(6):
                at = 4 * (f % 3) + t
                source = down if f < 3 else scaled
                left[f, base : base + 16] = jnp.broadcast_to(
                    source[:, at : at + 1], (TILE, TILE)
                ).reshape(16, 8, TILE)
    for f in range(6):
        left[f, 4 * PAD : 4 * PAD + 4] = jnp.full((4, 8, TILE), FAR if f < 3 else 0.0, F32)
    acc_left[...] = jnp.zeros_like(acc_left)
    acc_right[...] = jnp.zeros_like(acc_right)
    copy.wait()

    def turn(_, state):
        r, k = state
        for _ in range(UNROLL):
            b = ((list_s[k >> 2, r] >> ((k & 3) * 6)) & 63) * 4
            at = pl.ds(b, 4)
            rx, ry, rz, rq, re, rs_ = [
                jnp.broadcast_to(right[f, pl.ds(r, 1), :], (8, TILE))[None] for f in range(6)
            ]
            dx = left[0, at] - rx
            dy = left[1, at] - ry
            dz = left[2, at] - rz
            s2 = (dx * dx + 0.09) + dy * dy + dz * dz
            rs = lax.rsqrt(s2)
            inv = rs * rs
            screen = jnp.exp2(s2 * (-LOG2E) * rs)
            w = jnp.maximum(3.33 - s2, 0.0)
            slope = (w * inv) * 1.5
            one = slope + 1.0
            two = one + slope
            size = left[5, at] + rs_
            ratio = size * size * inv
            cubed = ratio * ratio * ratio
            lennard = (left[4, at] * re) * cubed * (cubed * two - one)
            coulomb = (left[3, at] * rq) * screen * (rs * (one + 5.0) + slope)
            g = (lennard + coulomb) * w
            fx, fy, fz = g * dx, g * dy, g * dz
            acc_left[0, at] += fx
            acc_left[1, at] += fy
            acc_left[2, at] += fz
            acc_right[0, r] -= jnp.sum(fx, axis=0)
            acc_right[1, r] -= jnp.sum(fy, axis=0)
            acc_right[2, r] -= jnp.sum(fz, axis=0)
            on = k + 1 >= list_s[12, r]
            k = jnp.where(on, 0, k + 1)
            r = jnp.where(on, r + 1, r)
        return r, k

    lax.fori_loop(0, (list_s[13, 0] + UNROLL - 1) // UNROLL, turn, (jnp.int32(0), jnp.int32(0)))
    tail = jnp.broadcast_to(weight, (4, TILE))

    def gathered(k):
        rows = [jnp.sum(acc_right[f, 4 * k : 4 * k + 4], axis=1) for f in range(3)]
        return jnp.concatenate(rows + [tail], 0)

    for k in range(NP):
        fout_ref[k] = gathered(k)
    ones = [
        jnp.where(lax.broadcasted_iota(jnp.int32, (2 * TILE, TILE), 1) == f, 1.0, 0.0).astype(BF16)
        for f in range(3)
    ]
    ones = jnp.concatenate(ones, 0)
    for box in range(3):
        parts = []
        for t in range(4):
            base = (t * 16 + box * 4) * 4
            halves = []
            for f in range(3):
                a = acc_left[f, base : base + 16].reshape(TILE, TILE)
                hi = a.astype(BF16)
                halves += [hi, (a - hi.astype(F32)).astype(BF16)]
            parts.append(jnp.concatenate(halves, 1))
        sums = jnp.dot(jnp.concatenate(parts, 0), ones, preferred_element_type=F32)
        target = fown_ref if box == 1 else fout_ref.at[NP if box == 0 else NP + 1]
        other = gathered(NP)
        for t in range(4):
            row = jnp.transpose(sums[TILE * t : TILE * t + TILE], (1, 0))
            for f in range(3):
                at = 4 * f + t
                value = row[f : f + 1]
                target[at : at + 1, :] = value + other[at : at + 1] if box == 1 else value
        target[12:16, :] = tail


def pair_forces(pos, par, own, joined):
    vmem = pl.BlockSpec(memory_space=pltpu.VMEM)
    return pl.pallas_call(
        functools.partial(pair_kernel, joined),
        out_shape=(
            jax.ShapeDtypeStruct((NBR, 16, TILE), F32),
            jax.ShapeDtypeStruct((16, TILE), F32),
        ),
        in_specs=[vmem] * 3,
        out_specs=(vmem, vmem),
        scratch_shapes=[
            pltpu.VMEM((6, 256, 8, TILE), F32),
            pltpu.VMEM((6, RROWS, TILE), F32),
            pltpu.VMEM((3, 256, 8, TILE), F32),
            pltpu.VMEM((3, RROWS, 8, TILE), F32),
            pltpu.VMEM((16, TILE), jnp.int32),
            pltpu.SMEM((16, TILE), jnp.int32),
            pltpu.SemaphoreType.DMA,
        ],
        compiler_params=pltpu.CompilerParams(vmem_limit_bytes=24 << 20),
    )(pos, par, own)


def hilbert(cells, bits):
    x = list(cells)
    q = 1 << (bits - 1)
    while q > 1:
        p = q - 1
        for i in range(3):
            hit = (x[i] & q) != 0
            if i == 0:
                x[0] = jnp.where(hit, x[0] ^ p, x[0])
            else:
                swap = (x[0] ^ x[i]) & p
                x[0], x[i] = jnp.where(hit, x[0] ^ p, x[0] ^ swap), jnp.where(hit, x[i], x[i] ^ swap)
        q >>= 1
    x[1] = x[1] ^ x[0]
    x[2] = x[2] ^ x[1]
    flip = jnp.zeros_like(x[0])
    q = 1 << (bits - 1)
    while q > 1:
        flip = jnp.where((x[2] & q) != 0, flip ^ (q - 1), flip)
        q >>= 1
    x = [v ^ flip for v in x]
    key = jnp.zeros_like(x[0])
    for bit in range(bits - 1, -1, -1):
        for a in range(3):
            key = key * 2 + ((x[a] >> bit) & 1)
    return key


def split3(a):
    hi = a.astype(BF16)
    rest = a - hi.astype(F32)
    mid = rest.astype(BF16)
    lo = (rest - mid.astype(F32)).astype(BF16)
    return jnp.concatenate([hi, mid, lo], 0)


def chosen(rank, t):
    place = lax.broadcasted_iota(jnp.int32, (TILE, TILE), 0) + TILE * t
    tiles = [(rank[j : j + 1, :] == place).astype(F32).astype(BF16) for j in range(4)]
    return jnp.concatenate(tiles, 1)


def there(offset, sign):
    return tuple(
        lax.rem(lax.axis_index(a) + sign * o + lax.axis_size(a), lax.axis_size(a))
        for a, o in zip(AXES, offset)
    )


def hail(offsets):
    barrier = pltpu.get_barrier_semaphore()
    for d in offsets:
        pl.semaphore_signal(barrier, inc=1, device_id=there(d, 1), device_id_type=MESH)


def meet(offsets):
    pl.semaphore_wait(pltpu.get_barrier_semaphore(), len(offsets))


def send(source, target, send_sem, recv_sem, device):
    return pltpu.make_async_remote_copy(
        src_ref=source,
        dst_ref=target,
        send_sem=send_sem,
        recv_sem=recv_sem,
        device_id=device,
        device_id_type=MESH,
    )


def first_kernel(*refs):
    given, (x_ref, v_ref, all_ref, rank_ref), held = refs[:8], refs[8:12], refs[12:20]
    stage, staged, rec, sem, send_sem, recv_sem = refs[20:]
    hail(OFFSETS)
    copies = [
        pltpu.make_async_copy(source, target, sem.at[i])
        for i, (source, target) in enumerate(zip(given, held))
    ]
    for copy in copies:
        copy.start()
    for copy in copies:
        copy.wait()
    pos_ref, vel_ref, frc_ref, chg_ref, typ_ref, count_ref, eps_ref, sig_ref = held

    def rows(ref, f):
        return [ref[f, 0, 0, :, TILE * t : TILE * t + TILE] for t in range(4)]

    def rows1(ref):
        return [ref[0, 0, :, TILE * t : TILE * t + TILE] for t in range(4)]

    def flat(ref):
        return jnp.concatenate([row for f in range(3) for row in rows(ref, f)], 0)

    v = flat(vel_ref) + HALF_STEP * flat(frc_ref)
    x = flat(pos_ref) + TIME_STEP * v
    count = count_ref[0, 0, 0]
    row = lax.broadcasted_iota(jnp.int32, (4, TILE), 0)
    live = row < count
    kinds = jnp.concatenate(rows1(typ_ref), 0)
    eps = jnp.zeros((4, TILE), F32)
    sig = jnp.zeros((4, TILE), F32)
    for k in range(eps_ref.shape[0]):
        eps = jnp.where(kinds == k, eps_ref[k], eps)
        sig = jnp.where(kinds == k, sig_ref[k], sig)
    alive = live.astype(F32)
    stage[...] = jnp.zeros_like(stage)
    stage[0:12, :] = x
    stage[12:24, :] = v
    stage[24:28, :] = jnp.concatenate(rows1(chg_ref), 0) * alive
    stage[28:32, :] = jnp.sqrt(eps) * alive
    stage[32:36, :] = sig
    cells = [
        jnp.clip((jnp.clip(x[4 * a : 4 * a + 4], -1.0, 2.0) * 4.0).astype(jnp.int32), 0, 3)
        for a in range(3)
    ]
    index = row * TILE + lax.broadcasted_iota(jnp.int32, (4, TILE), 1)
    key = jnp.where(live, hilbert(cells, 2), 64) * 512 + index
    key = jnp.concatenate([key.astype(F32), jnp.zeros((4, TILE), F32)], 0)
    down = jnp.transpose(key, (1, 0))
    ranks = []
    for j in range(4):
        less = jnp.zeros((TILE, TILE), F32)
        for i in range(4):
            less = less + (down[:, i : i + 1] < key[j : j + 1, :]).astype(F32)
        ranks.append(jnp.sum(less, axis=0, keepdims=True))
    rank = jnp.concatenate(ranks, 0).astype(jnp.int32)
    rank_ref[...] = rank
    fields = jnp.concatenate([stage[pl.ds(t, 16, stride=4), :] for t in range(4)], 1)
    parts = split3(fields)
    for t in range(4):
        out = lax.dot_general(
            parts, chosen(rank, t), (((1,), (1,)), ((), ())), preferred_element_type=F32
        )
        staged[pl.ds(t, 16, stride=4), :] = (out[32:48] + out[16:32]) + out[0:16]
    row16 = lax.broadcasted_iota(jnp.int32, (16, TILE), 0)
    place = staged[0:16, :]
    x_ref[...] = place
    v_ref[...] = staged[12:28, :]
    rec[0] = jnp.where((row16 & 3) < count, place, FAR)
    rec[1] = jnp.where(row16 < 12, staged[24:40, :], count.astype(F32))
    meet(OFFSETS)
    copies = [
        send(rec, all_ref.at[k], send_sem.at[k], recv_sem.at[k], there(d, -1))
        for k, d in enumerate(OFFSETS)
    ]
    for copy in copies:
        copy.start()
    own = pltpu.make_async_copy(rec, all_ref.at[NBR], sem.at[8])
    own.start()
    own.wait()
    for copy in copies:
        copy.wait()


def turn_kernel(
    fout_ref, fown_ref, x_ref, v_ref, old_ref,
    nbr_ref, new_ref, x2_ref, v2_ref,
    back, send_sem, recv_sem, send2_sem, recv2_sem,
):
    hail(OFFSETS)
    meet(OFFSETS)
    copies = [
        send(fout_ref.at[k], back.at[k], send_sem.at[k], recv_sem.at[k], there(d, 1))
        for k, d in enumerate(OFFSETS)
    ]
    for copy in copies:
        copy.start()
    for copy in copies:
        copy.wait_recv()
    total = fown_ref[...]
    for k in range(NBR):
        total = total + back[k]
    v = v_ref[...] + HALF_STEP * total
    v = v + HALF_STEP * total
    x = x_ref[...] + TIME_STEP * v
    row16 = lax.broadcasted_iota(jnp.int32, (16, TILE), 0)
    new = jnp.where(old_ref[NBR, 0] > 0.1 * FAR, FAR, x)
    new = jnp.where(row16 == 12, back[NP + 1, 12:13, :], new)
    new = jnp.where(row16 == 13, back[NP, 12:13, :], new)
    new_ref[...] = jnp.where(row16 == 14, fown_ref[12:13, :], new)
    again = [
        send(new_ref, nbr_ref.at[k], send2_sem.at[k], recv2_sem.at[k], there(d, -1))
        for k, d in enumerate(OFFSETS)
    ]
    for copy in again:
        copy.start()
    x2_ref[...] = x
    v2_ref[...] = v
    for copy in copies:
        copy.wait_send()
    for copy in again:
        copy.wait()


def last_kernel(
    fout_ref, fown_ref, x_ref, v_ref, rank_ref, xo_ref, vo_ref, fo_ref,
    back, stage, onehot, send_sem, recv_sem,
):
    hail(OFFSETS)
    meet(OFFSETS)
    copies = [
        send(fout_ref.at[k], back.at[k], send_sem.at[k], recv_sem.at[k], there(d, 1))
        for k, d in enumerate(OFFSETS)
    ]
    for copy in copies:
        copy.start()
    rank = rank_ref[...]
    for t in range(4):
        onehot[TILE * t : TILE * t + TILE, :] = chosen(rank, t)
    for copy in copies:
        copy.wait()
    total = fown_ref[...]
    for k in range(NBR):
        total = total + back[k]
    stage[0:16, :] = x_ref[...]
    stage[12:28, :] = v_ref[...] + HALF_STEP * total
    stage[24:40, :] = total
    stage[36:64, :] = jnp.zeros((28, TILE), F32)
    fields = jnp.concatenate([stage[pl.ds(t, 16, stride=4), :] for t in range(4)], 1)
    out = jnp.dot(split3(fields), onehot[...], preferred_element_type=F32)
    out = (out[32:48] + out[16:32]) + out[0:16]
    for f in range(3):
        xo_ref[f, 0, 0] = out[f : f + 1]
        vo_ref[f, 0, 0] = out[3 + f : 4 + f]
        fo_ref[f, 0, 0] = out[6 + f : 7 + f]


def place_kernel(*refs):
    copies = [pltpu.make_async_copy(refs[i], refs[3 + i], refs[6].at[i]) for i in range(3)]
    for copy in copies:
        copy.start()
    for copy in copies:
        copy.wait()


def call(kernel, outs, scratch, collective=None, ins=None, raw_in=False, raw_out=False, limit=24 << 20):
    vmem = pl.BlockSpec(memory_space=pltpu.VMEM)
    hbm = pl.BlockSpec(memory_space=pltpu.HBM)
    params = {"vmem_limit_bytes": limit}
    if collective is not None:
        params.update(collective_id=collective, has_side_effects=True)
    return pl.pallas_call(
        kernel,
        out_shape=tuple(jax.ShapeDtypeStruct(shape, kind) for shape, kind in outs),
        in_specs=[hbm if raw_in else vmem] * ins,
        out_specs=tuple(hbm if raw_out else vmem for _ in outs),
        scratch_shapes=scratch,
        compiler_params=pltpu.CompilerParams(**params),
    )


def on_device(
    positions, velocities, forces, charges, atom_types, tile_counts, pair_epsilon, pair_sigma
):
    dma = pltpu.SemaphoreType.DMA((NBR,))
    rows = ((16, TILE), F32)
    wide = (positions, velocities, forces, charges, atom_types)
    small = (tile_counts, pair_epsilon, pair_sigma)
    x, v, first, rank = call(
        first_kernel,
        (rows, rows, ((NBR + 1, 2, 16, TILE), F32), ((4, TILE), jnp.int32)),
        [pltpu.VMEM(given.shape, given.dtype) for given in wide]
        + [pltpu.SMEM(given.shape, given.dtype) for given in small]
        + [pltpu.VMEM((64, TILE), F32), pltpu.VMEM((64, TILE), F32), pltpu.VMEM((2, 16, TILE), F32),
           pltpu.SemaphoreType.DMA((9,)), dma, dma],
        collective=0,
        ins=8,
        raw_in=True,
        limit=67043328,
    )(
        *wide, *small
    )
    fout, fown = pair_forces(first, first, first, True)
    second, own, x, v = call(
        turn_kernel,
        (((NBR, 16, TILE), F32), rows, rows, rows),
        [pltpu.VMEM((NBR, 16, TILE), F32), dma, dma, dma, dma],
        collective=1,
        ins=5,
    )(fout, fown, x, v, first)
    fout, fown = pair_forces(second, first, own, False)
    flat = ((3, 1, 1, 1, 4 * TILE), F32)
    outs = call(
        last_kernel,
        (flat, flat, flat),
        [pltpu.VMEM((NBR, 16, TILE), F32), pltpu.VMEM((64, TILE), F32),
         pltpu.VMEM((512, 512), BF16), dma, dma],
        collective=2,
        ins=5,
    )(fout, fown, x, v, rank)
    return call(
        place_kernel, (flat, flat, flat), [pltpu.SemaphoreType.DMA((3,))], ins=3, raw_out=True
    )(*outs)


def solution(mesh):
    atoms = P(None, "gx", "gy", "gz", None)
    in_specs = (
        atoms, atoms, atoms,
        P("gx", "gy", "gz", None),
        P("gx", "gy", "gz", None),
        P("gx", "gy", "gz"),
        P(), P(),
    )
    return jax.shard_map(
        on_device, mesh=mesh, in_specs=in_specs, out_specs=(atoms,) * 3, check_vma=False
    )
```

profile of v0, /device:TPU:2, one launch (start us, length us, event | category | flops | bytes accessed | tf_op | source)
XLA Modules:
  0.0 80.1 jit_solution(17775836295994323024)
XLA Ops:
  1.3 24.8 %shard_map.103 = (f32[16,128]{1,0:T(8,128)}, f32[16,128]{1,0:T(8,128)}, f32[11,2,16,128]{3,2,1,0:T(8,128)}, s32[4,128]{1,0:T(4,128)}) custom-call(f32[3,1,1,1,512]{4,3,2,1,0:T(1,128)} %refs_0_.1, f32[3,1,1,1,512]{4,3,2,1,0:T(1,128)} %refs_1_.1, f32[3,1,1,1,512]{4,3,2,1,0:T(1,128)} %refs_2_.1, f32[1,1,1,512]{3,2,1,0:T(1,128)} %refs_3_.1, ...), custom_call_target="tpu_custom_call" | custom-call | tf_op jit(solution)/shard_map/pallas_call | solution.py:526
  26.1 0.0 copy-start
  26.1 0.9 %copy-done = f32[11,2,16,128]{3,2,1,0:T(8,128)S(1)} copy-done((f32[11,2,16,128]{3,2,1,0:T(8,128)S(1)}, f32[11,2,16,128]{3,2,1,0:T(8,128)}, u32[]{:S(2)}) %copy-start) | copy-done | bytes 180248
  27.0 0.0 copy-start.1
  27.0 0.0 copy-start.2
  27.0 0.0 copy-start.3
  27.0 13.4 %shard_map.104 = (f32[10,16,128]{2,1,0:T(8,128)S(1)}, f32[16,128]{1,0:T(8,128)S(1)}) custom-call(f32[11,2,16,128]{3,2,1,0:T(8,128)S(1)} %copy-done, f32[11,2,16,128]{3,2,1,0:T(8,128)S(1)} %copy-done, f32[11,2,16,128]{3,2,1,0:T(8,128)S(1)} %copy-done), custom_call_target="tpu_custom_call" | custom-call | tf_op jit(solution)/shard_map/pallas_call | solution.py:247
  40.5 0.0 copy-done.1
  40.5 0.0 copy-done.2
  40.5 0.0 copy-done.3
  40.5 15.0 %shard_map.105 = (f32[10,16,128]{2,1,0:T(8,128)S(1)}, f32[16,128]{1,0:T(8,128)S(1)}, f32[16,128]{1,0:T(8,128)S(1)}, f32[16,128]{1,0:T(8,128)S(1)}) custom-call(f32[10,16,128]{2,1,0:T(8,128)S(1)} %get-tuple-element.19.fout_ref, f32[16,128]{1,0:T(8,128)S(1)} %get-tuple-element.20.fown_ref, f32[16,128]{1,0:T(8,128)S(1)} %copy-done.2, f32[16,128]{1,0:T(8,128)S(1)} %copy-done.3, ...), custom_call_target="tpu_custom_call" | custom-call | tf_op jit(solution)/shard_map/pallas_call | solution.py:541
  55.4 12.5 %shard_map.106 = (f32[10,16,128]{2,1,0:T(8,128)S(1)}, f32[16,128]{1,0:T(8,128)S(1)}) custom-call(f32[10,16,128]{2,1,0:T(8,128)S(1)} %get-tuple-element.23.pos_ref, f32[11,2,16,128]{3,2,1,0:T(8,128)S(1)} %copy-done.1, f32[16,128]{1,0:T(8,128)S(1)} %get-tuple-element.24.own_ref), custom_call_target="tpu_custom_call" | custom-call | tf_op jit(solution)/shard_map/pallas_call | solution.py:247
  68.0 0.0 copy-start.4
  68.0 0.7 copy-done.4
  68.7 10.8 %shard_map.107 = (f32[3,1,1,1,512]{4,3,2,1,0:T(1,128)S(1)}, f32[3,1,1,1,512]{4,3,2,1,0:T(1,128)S(1)}, f32[3,1,1,1,512]{4,3,2,1,0:T(1,128)S(1)}) custom-call(f32[10,16,128]{2,1,0:T(8,128)S(1)} %get-tuple-element.25.fout_ref, f32[16,128]{1,0:T(8,128)S(1)} %get-tuple-element.26.fown_ref, f32[16,128]{1,0:T(8,128)S(1)} %get-tuple-element.27.x_ref, ...), custom_call_target="tpu_custom_call" | custom-call | tf_op jit(solution)/shard_map/pallas_call | solution.py:550
  79.5 0.6 shard_map.108
Async XLA Ops:
  26.1 0.9 %copy-start = (f32[11,2,16,128]{3,2,1,0:T(8,128)S(1)}, f32[11,2,16,128]{3,2,1,0:T(8,128)}, u32[]{:S(2)}) copy-start(f32[11,2,16,128]{3,2,1,0:T(8,128)} %get-tuple-element.18.pos_ref.par_ref.own_ref.old_ref) | copy-start | bytes 540676
  27.0 13.5 %copy-start.1 = (f32[11,2,16,128]{3,2,1,0:T(8,128)S(1)}, f32[11,2,16,128]{3,2,1,0:T(8,128)}, u32[]{:S(2)}) copy-start(f32[11,2,16,128]{3,2,1,0:T(8,128)} %get-tuple-element.18.pos_ref.par_ref.own_ref.old_ref) | copy-start | bytes 540676
  27.0 13.5 %copy-start.2 = (f32[16,128]{1,0:T(8,128)S(1)}, f32[16,128]{1,0:T(8,128)}, u32[]{:S(2)}) copy-start(f32[16,128]{1,0:T(8,128)} %get-tuple-element.21.x_ref) | copy-start | bytes 24580
  27.0 13.5 %copy-start.3 = (f32[16,128]{1,0:T(8,128)S(1)}, f32[16,128]{1,0:T(8,128)}, u32[]{:S(2)}) copy-start(f32[16,128]{1,0:T(8,128)} %get-tuple-element.22.v_ref) | copy-start | bytes 24580
  68.0 0.7 copy-start.4
where the time goes:
time: 80 us; the launch traced here: 80.1 us
  Pallas kernels  77.1 us (96%)
  local copies, waits for them, and re-layouts  1.58 us (2%)
  between operations  1.36 us (2%)
    pallas_call x2, Pallas kernels, pair_forces(): pl.pallas_call(functools.partial(pair_kernel, joined), out_shape=(jax.Sha...  26 us
    pallas_call x1, Pallas kernels, on_device(): call(first_kernel, (rows, rows, ((NBR + 1, 2, 16, TILE), F32), ((4, TILE)...  24.8 us
    pallas_call x1, Pallas kernels, on_device(): call(turn_kernel, (((NBR, 16, TILE), F32), rows, rows, rows), [pltpu.VMEM...  15 us
    pallas_call x1, Pallas kernels, on_device(): call(last_kernel, (flat, flat, flat), [pltpu.VMEM((NBR, 16, TILE), F32),...  10.8 us

commit v1 on v0

--- a/solution.py
+++ b/solution.py
@@ -153,16 +153,22 @@
     list_v[13:14, :] = jnp.broadcast_to(total, (1, TILE)).astype(jnp.int32)
     copy = pltpu.make_async_copy(list_v, list_s, sem)
     copy.start()
+    wanted = (lax.broadcasted_iota(jnp.int32, (48, 4 * TILE), 0) & 15) - (
+        lax.broadcasted_iota(jnp.int32, (48, 4 * TILE), 1) >> 7
+    )
+    picks = [jnp.where(wanted == 4 * f, 1.0, 0.0).astype(BF16) for f in range(3)]
     for box, down in enumerate(downs):
         scaled = down[:, 16:] * scale
-        for t in range(4):
-            base = (t * 16 + box * 4) * 4
-            for f in range(6):
-                at = 4 * (f % 3) + t
-                source = down if f < 3 else scaled
-                left[f, base : base + 16] = jnp.broadcast_to(
-                    source[:, at : at + 1], (TILE, TILE)
-                ).reshape(16, 8, TILE)
+        for f in range(0, 6):
+            source = down[:, :16] if f < 3 else scaled
+            hi = source.astype(BF16)
+            rest = source - hi.astype(F32)
+            mid = rest.astype(BF16)
+            pieces = jnp.concatenate([hi, mid, (rest - mid.astype(F32)).astype(BF16)], 1)
+            wide = jnp.dot(pieces, picks[f % 3], preferred_element_type=F32)
+            for t in range(4):
+                base = (t * 16 + box * 4) * 4
+                left[f, base : base + 16] = wide[:, TILE * t : TILE * t + TILE].reshape(16, 8, TILE)
     for f in range(6):
         left[f, 4 * PAD : 4 * PAD + 4] = jnp.full((4, 8, TILE), FAR if f < 3 else 0.0, F32)
     acc_left[...] = jnp.zeros_like(acc_left)
@@ -302,7 +308,7 @@
 
 
 def chosen(rank, t):
-    place = lax.broadcasted_iota(jnp.int32, (TILE, TILE), 0) + TILE * t
+    place = (lax.broadcasted_iota(jnp.int32, (TILE, TILE), 0) + TILE * t).astype(F32)
     tiles = [(rank[j : j + 1, :] == place).astype(F32).astype(BF16) for j in range(4)]
     return jnp.concatenate(tiles, 1)
 
@@ -336,8 +342,8 @@
 
 
 def first_kernel(*refs):
-    given, (x_ref, v_ref, all_ref, rank_ref), held = refs[:8], refs[8:12], refs[12:20]
-    stage, staged, rec, sem, send_sem, recv_sem = refs[20:]
+    given, (x_ref, v_ref, all_ref), held = refs[:8], refs[8:11], refs[11:19]
+    stage, staged, rec, sem, send_sem, recv_sem = refs[19:]
     hail(OFFSETS)
     copies = [
         pltpu.make_async_copy(source, target, sem.at[i])
@@ -390,8 +396,7 @@
         for i in range(4):
             less = less + (down[:, i : i + 1] < key[j : j + 1, :]).astype(F32)
         ranks.append(jnp.sum(less, axis=0, keepdims=True))
-    rank = jnp.concatenate(ranks, 0).astype(jnp.int32)
-    rank_ref[...] = rank
+    rank = jnp.concatenate(ranks, 0)
     fields = jnp.concatenate([stage[pl.ds(t, 16, stride=4), :] for t in range(4)], 1)
     parts = split3(fields)
     for t in range(4):
@@ -404,6 +409,7 @@
     x_ref[...] = place
     v_ref[...] = staged[12:28, :]
     rec[0] = jnp.where((row16 & 3) < count, place, FAR)
+    rec[0, 12:16, :] = rank
     rec[1] = jnp.where(row16 < 12, staged[24:40, :], count.astype(F32))
     meet(OFFSETS)
     copies = [
@@ -460,7 +466,7 @@
 
 
 def last_kernel(
-    fout_ref, fown_ref, x_ref, v_ref, rank_ref, xo_ref, vo_ref, fo_ref,
+    fout_ref, fown_ref, x_ref, v_ref, first_ref, xo_ref, vo_ref, fo_ref,
     back, stage, onehot, send_sem, recv_sem,
 ):
     hail(OFFSETS)
@@ -471,7 +477,7 @@
     ]
     for copy in copies:
         copy.start()
-    rank = rank_ref[...]
+    rank = first_ref[NBR, 0, 12:16, :]
     for t in range(4):
         onehot[TILE * t : TILE * t + TILE, :] = chosen(rank, t)
     for copy in copies:
@@ -523,9 +529,9 @@
     rows = ((16, TILE), F32)
     wide = (positions, velocities, forces, charges, atom_types)
     small = (tile_counts, pair_epsilon, pair_sigma)
-    x, v, first, rank = call(
+    x, v, first = call(
         first_kernel,
-        (rows, rows, ((NBR + 1, 2, 16, TILE), F32), ((4, TILE), jnp.int32)),
+        (rows, rows, ((NBR + 1, 2, 16, TILE), F32)),
         [pltpu.VMEM(given.shape, given.dtype) for given in wide]
         + [pltpu.SMEM(given.shape, given.dtype) for given in small]
         + [pltpu.VMEM((64, TILE), F32), pltpu.VMEM((64, TILE), F32), pltpu.VMEM((2, 16, TILE), F32),
@@ -554,7 +560,7 @@
          pltpu.VMEM((512, 512), BF16), dma, dma],
         collective=2,
         ins=5,
-    )(fout, fown, x, v, rank)
+    )(fout, fown, x, v, first)
     return call(
         place_kernel, (flat, flat, flat), [pltpu.SemaphoreType.DMA((3,))], ins=3, raw_out=True
     )(*outs)

time: 80 us -> 78.1 us (0.976)
  the two profiles are of different devices: /device:TPU:2 before, /device:TPU:4 now
where the time goes in v1:
time: 78.1 us; the launch traced here: 79 us
  Pallas kernels  76.7 us (98%)
  between operations  1.35 us (2%)
  local copies, waits for them, and re-layouts  0.93 us (1%)
    pallas_call x1, Pallas kernels, on_device(): call(first_kernel, (rows, rows, ((NBR + 1, 2, 16, TILE), F32)), [pltpu.VM...  24.8 us
    pallas_call x2, Pallas kernels, pair_forces(): pl.pallas_call(functools.partial(pair_kernel, joined), out_shape=(jax.Sha...  23.1 us
    pallas_call x1, Pallas kernels, on_device(): call(turn_kernel, (((NBR, 16, TILE), F32), rows, rows, rows), [pltpu.VMEM...  17.2 us
    pallas_call x1, Pallas kernels, on_device(): call(last_kernel, (flat, flat, flat), [pltpu.VMEM((NBR, 16, TILE), F32),...  11 us

profile of v1, /device:TPU:4, one launch (start us, length us, event | category | flops | bytes accessed | tf_op | source)
XLA Modules:
  0.0 79.0 jit_solution(12928632208138388222)
XLA Ops:
  1.3 24.8 %shard_map.103 = (f32[16,128]{1,0:T(8,128)}, f32[16,128]{1,0:T(8,128)}, f32[11,2,16,128]{3,2,1,0:T(8,128)}) custom-call(f32[3,1,1,1,512]{4,3,2,1,0:T(1,128)} %refs_0_.1, f32[3,1,1,1,512]{4,3,2,1,0:T(1,128)} %refs_1_.1, f32[3,1,1,1,512]{4,3,2,1,0:T(1,128)} %refs_2_.1, f32[1,1,1,512]{3,2,1,0:T(1,128)} %refs_3_.1, s32[1,1,1,512]{3,2,1,0:T(1,128)} %refs_4_.1, ...), custom_call_target="tpu_custom_call" | custom-call | tf_op jit(solution)/shard_map/pallas_call | solution.py:532
  26.1 0.0 copy-start
  26.1 0.9 %copy-done = f32[11,2,16,128]{3,2,1,0:T(8,128)S(1)} copy-done((f32[11,2,16,128]{3,2,1,0:T(8,128)S(1)}, f32[11,2,16,128]{3,2,1,0:T(8,128)}, u32[]{:S(2)}) %copy-start) | copy-done | bytes 180248
  27.0 0.0 copy-start.1
  27.0 0.0 copy-start.2
  27.0 0.0 copy-start.3
  27.0 11.1 %shard_map.104 = (f32[10,16,128]{2,1,0:T(8,128)S(1)}, f32[16,128]{1,0:T(8,128)S(1)}) custom-call(f32[11,2,16,128]{3,2,1,0:T(8,128)S(1)} %copy-done, f32[11,2,16,128]{3,2,1,0:T(8,128)S(1)} %copy-done, f32[11,2,16,128]{3,2,1,0:T(8,128)S(1)} %copy-done), custom_call_target="tpu_custom_call" | custom-call | tf_op jit(solution)/shard_map/pallas_call | solution.py:253
  38.1 0.0 copy-done.1
  38.1 0.0 copy-done.2
  38.1 0.0 copy-done.3
  38.1 17.2 %shard_map.105 = (f32[10,16,128]{2,1,0:T(8,128)S(1)}, f32[16,128]{1,0:T(8,128)S(1)}, f32[16,128]{1,0:T(8,128)S(1)}, f32[16,128]{1,0:T(8,128)S(1)}) custom-call(f32[10,16,128]{2,1,0:T(8,128)S(1)} %get-tuple-element.18.fout_ref, f32[16,128]{1,0:T(8,128)S(1)} %get-tuple-element.19.fown_ref, f32[16,128]{1,0:T(8,128)S(1)} %copy-done.2, f32[16,128]{1,0:T(8,128)S(1)} %copy-done.3, ...), custom_call_target="tpu_custom_call" | custom-call | tf_op jit(solution)/shard_map/pallas_call | solution.py:547
  55.4 12.0 %shard_map.106 = (f32[10,16,128]{2,1,0:T(8,128)S(1)}, f32[16,128]{1,0:T(8,128)S(1)}) custom-call(f32[10,16,128]{2,1,0:T(8,128)S(1)} %get-tuple-element.22.pos_ref, f32[11,2,16,128]{3,2,1,0:T(8,128)S(1)} %copy-done.1, f32[16,128]{1,0:T(8,128)S(1)} %get-tuple-element.23.own_ref), custom_call_target="tpu_custom_call" | custom-call | tf_op jit(solution)/shard_map/pallas_call | solution.py:253
  67.3 11.0 %shard_map.107 = (f32[3,1,1,1,512]{4,3,2,1,0:T(1,128)S(1)}, f32[3,1,1,1,512]{4,3,2,1,0:T(1,128)S(1)}, f32[3,1,1,1,512]{4,3,2,1,0:T(1,128)S(1)}) custom-call(f32[10,16,128]{2,1,0:T(8,128)S(1)} %get-tuple-element.24.fout_ref, f32[16,128]{1,0:T(8,128)S(1)} %get-tuple-element.25.fown_ref, f32[16,128]{1,0:T(8,128)S(1)} %get-tuple-element.26.x_ref, ...), custom_call_target="tpu_custom_call" | custom-call | tf_op jit(solution)/shard_map/pallas_call | solution.py:556
  78.4 0.6 shard_map.108
Async XLA Ops:
  26.1 0.9 %copy-start = (f32[11,2,16,128]{3,2,1,0:T(8,128)S(1)}, f32[11,2,16,128]{3,2,1,0:T(8,128)}, u32[]{:S(2)}) copy-start(f32[11,2,16,128]{3,2,1,0:T(8,128)} %get-tuple-element.17.pos_ref.par_ref.own_ref.old_ref.first_ref) | copy-start | bytes 540676
  27.0 11.1 %copy-start.1 = (f32[11,2,16,128]{3,2,1,0:T(8,128)S(1)}, f32[11,2,16,128]{3,2,1,0:T(8,128)}, u32[]{:S(2)}) copy-start(f32[11,2,16,128]{3,2,1,0:T(8,128)} %get-tuple-element.17.pos_ref.par_ref.own_ref.old_ref.first_ref) | copy-start | bytes 540676
  27.0 11.1 %copy-start.2 = (f32[16,128]{1,0:T(8,128)S(1)}, f32[16,128]{1,0:T(8,128)}, u32[]{:S(2)}) copy-start(f32[16,128]{1,0:T(8,128)} %get-tuple-element.20.x_ref) | copy-start | bytes 24580
  27.0 11.1 %copy-start.3 = (f32[16,128]{1,0:T(8,128)S(1)}, f32[16,128]{1,0:T(8,128)}, u32[]{:S(2)}) copy-start(f32[16,128]{1,0:T(8,128)} %get-tuple-element.21.v_ref) | copy-start | bytes 24580
